TPU v7x, 32 devices: a whole 2x2x4 slice. The times are simulated.
32 devices in a mesh: dp: 8 (over y, x, core), mp: 4 (over z).
Axes of the slice: x: 2, y: 2, z: 4, core: 2. Of those that a mesh axis runs over, the one named last changes fastest.
Arguments:
- patches: bfloat16 [1024, 588], P('dp'), may hold values from -6 to 6
- embed_weight: bfloat16 [6144, 588], P(('mp', 'dp')), may hold values from -0.25 to 0.25
- project_weight: bfloat16 [6144, 3, 3072], P('dp', None, 'mp'), may hold values from -0.078125 to 0.078125
- patch_counts: int32 [64], P('dp'), may hold values from 0 to 64, as said below
- segment_ids: int32 [1024], P('dp'), may hold values from -1 to 63, as said below
- targets: bfloat16 [1024, 3072], P('dp', 'mp'), may hold values from -4 to 4
Outputs:
- project_grad: float32 [6144, 3, 3072], P('dp', None, 'mp')
- loss_value: float32 [], replicated
Inputs may be any that keep to these rules, and one draw needn't show every extreme that they name: `patch_counts`: entry 8 * i + j is the number of patches of image slot j of device i along dp, a multiple of 16, 0 for an empty slot; the counts of one device add up to at most 128, and some device reaches it. `segment_ids`: the rows of device i along dp hold its images whole, slot after slot, each row carrying the id 8 * i + slot of its image, then -1 on the rows left. A device in the upper half of dp holds more rows than the device half the axis away. On each device the images that end after its row 96 cover at most 64 rows. Those rows plus all the rows of the device half the axis away come to at most 96. Both bounds are reached.
All inputs are finite; a program needn't handle non-finite values.
Results may differ from a plain program's by a relative error of at most 0.012.
The roundings to bfloat16 on the way count: a program that leaves them out, or rounds other values in their place, can miss the bound.
Values may be sent and summed in bfloat16 or wider, within the bound.
A program may use at most 128 MiB of HBM per device.

v0:
```python
import math

import jax
import jax.numpy as jnp
from jax import lax
from jax.sharding import PartitionSpec as P

HD = 128


def layer_norm(values):
    center = values - jnp.mean(values, axis=-1, keepdims=True)
    spread = jnp.mean(center * center, axis=-1, keepdims=True)
    return center * lax.rsqrt(spread + 1e-06)


def norm_grad(values, cotangent):
    return jax.vjp(layer_norm, values)[1](cotangent)[0]


def attend_block(query_raw, key_raw, value_rows, segment, target):
    inverse_root = 1.0 / math.sqrt(HD)
    query_normed = layer_norm(query_raw).astype(jnp.bfloat16)
    key_normed = layer_norm(key_raw).astype(jnp.bfloat16)
    scores = (
        jnp.einsum("qhd,khd->hqk", query_normed, key_normed, preferred_element_type=jnp.float32)
        * inverse_root
    )
    valid = segment >= 0
    allowed = (segment[:, None] == segment[None, :]) & valid[:, None]
    exponent = jnp.where(allowed[None], jnp.exp(scores), 0.0)
    denominator = jnp.sum(exponent, axis=-1, keepdims=True)
    denominator = jnp.where(valid[None, :, None], denominator, 1.0)
    weights = (exponent / denominator).astype(jnp.bfloat16)
    attended = jnp.einsum("hqk,khd->qhd", weights, value_rows, preferred_element_type=jnp.float32)
    feature_count = attended.shape[1] * attended.shape[2]
    error_rows = jnp.where(
        valid[:, None], attended.reshape(-1, feature_count) - target.astype(jnp.float32), 0.0
    )
    squared_sum = jnp.sum(error_rows * error_rows)
    return (query_normed, key_normed, weights, error_rows, squared_sum)


def attend_back(
    query_raw, key_raw, query_normed, key_normed, value_rows, weights, error_rows, patch_total
):
    inverse_root = 1.0 / math.sqrt(HD)
    out_grad = (error_rows / patch_total).astype(jnp.bfloat16).reshape(query_normed.shape)
    prob_grad = jnp.einsum("qhd,khd->hqk", out_grad, value_rows, preferred_element_type=jnp.float32)
    value_grad = jnp.einsum(
        "hqk,qhd->khd", weights, out_grad, preferred_element_type=jnp.float32
    ).astype(jnp.bfloat16)
    weight_float = weights.astype(jnp.float32)
    score_grad = (
        weight_float
        * (prob_grad - jnp.sum(prob_grad * weight_float, axis=-1, keepdims=True))
        * inverse_root
    ).astype(jnp.bfloat16)
    normed_grad_q = jnp.einsum(
        "hqk,khd->qhd", score_grad, key_normed, preferred_element_type=jnp.float32
    )
    normed_grad_k = jnp.einsum(
        "hqk,qhd->khd", score_grad, query_normed, preferred_element_type=jnp.float32
    )
    query_grad = norm_grad(query_raw, normed_grad_q).astype(jnp.bfloat16)
    key_grad = norm_grad(key_raw, normed_grad_k).astype(jnp.bfloat16)
    return jnp.stack([query_grad, key_grad, value_grad], axis=1)


def local(patches, embed_weight, project_weight, patch_counts, segment_ids, targets):
    local_total = jnp.sum(patch_counts).astype(jnp.float32)
    patch_total = lax.psum(local_total, "dp")
    row_total = patches.shape[0]
    own_features = jnp.einsum(
        "rp,cp->rc",
        patches,
        lax.all_gather(embed_weight, "dp", axis=0, tiled=True),
        preferred_element_type=jnp.float32,
    ).astype(jnp.bfloat16)
    embedded = lax.all_gather(own_features, "mp", axis=1, tiled=True)
    normed = layer_norm(embedded.astype(jnp.float32)).astype(jnp.bfloat16)
    flat_weight = project_weight.reshape(project_weight.shape[0], -1)
    section = normed
    projected = jnp.dot(
        section,
        lax.all_gather(flat_weight, "dp", axis=0, tiled=True),
        preferred_element_type=jnp.float32,
    )
    head_dev = project_weight.shape[2] // HD
    projected = projected.reshape(row_total, 3, head_dev, HD)
    query_raw = projected[:, 0]
    key_raw = projected[:, 1]
    value_rows = projected[:, 2].astype(jnp.bfloat16)
    query_normed, key_normed, weights, error_rows, squared_sum = attend_block(
        query_raw, key_raw, value_rows, segment_ids, targets
    )
    loss_value = lax.psum(squared_sum, ("dp", "mp")) / (2.0 * patch_total)
    grad_rows = attend_back(
        query_raw, key_raw, query_normed, key_normed, value_rows, weights, error_rows, patch_total
    )
    grad_rows = grad_rows.reshape(row_total, -1)
    normed_blocks = lax.all_to_all(normed, "dp", split_axis=1, concat_axis=0, tiled=True)
    section = normed_blocks
    weight_grad = lax.dot_general(
        section,
        lax.all_gather(grad_rows, "dp", axis=0, tiled=True),
        (((0,), (0,)), ((), ())),
        preferred_element_type=jnp.float32,
    )
    return (weight_grad.reshape(weight_grad.shape[0], 3, -1), loss_value)


def solution(mesh):
    in_specs = (
        P("dp", None),
        P(("mp", "dp"), None),
        P("dp", None, "mp"),
        P("dp"),
        P("dp"),
        P("dp", "mp"),
    )
    out_specs = (P("dp", None, "mp"), P())
    return jax.shard_map(local, mesh=mesh, in_specs=in_specs, out_specs=out_specs, check_vma=False)
```

profile of v0, /device:TPU:0, one launch (start us, length us, event | category | flops | bytes accessed | tf_op | source)
XLA Modules:
  0.0 322.9 jit_solution(9939542595625254220)
XLA Ops:
  7.2 0.7 all-gather.5.cloned.1.call-update
  8.0 31.9 %all-gather.5.cloned.1.call-done = bf16[1536,588]{1,0:T(8,128)(2,1)} async-done(((bf16[192,588]{1,0:T(8,128)(2,1)}), bf16[1536,588]{1,0:T(8,128)(2,1)}) %all-gather.5.cloned.1.call-update) | async-done | bytes 1806352 | tf_op jit(solution)/shard_map/all_gather | solution.py:77
  39.9 3.1 convolution_convert_fusion
  43.0 6.0 %copy.36 = bf16[768,3,768]{0,2,1:T(8,128)(2,1)} copy(bf16[768,3,768]{2,0,1:T(8,128)(2,1)} %param.8) | data formatting | bytes 7077888 | tf_op args[2]
  49.1 0.6 copy-done.6
  49.7 0.6 reduce_sum.134
  51.0 14.4 %psum.14 = f32[]{:T(128)} all-reduce(f32[]{:T(128)S(6)} %convert_element_type.58), channel_id=1, replica_groups=mesh['dp'=8,'mp'=4] {'dp'}, use_global_device_ids=true, to_apply=%region_8.9 | all-reduce | flops 1 | bytes 8 | tf_op jit(solution)/shard_map/psum | solution.py:72
  65.7 14.5 %all-gather.7.cloned.1.call-done = bf16[128,6144]{1,0:T(8,128)(2,1)} async-done(((bf16[128,1536]{1,0:T(8,128)(2,1)}), bf16[128,6144]{1,0:T(8,128)(2,1)}) %all-gather.7.cloned.1.call-update) | async-done | bytes 1572880 | tf_op jit(solution)/shard_map/all_gather | solution.py:80
  80.2 1.8 convert_reduce_fusion
  82.0 0.6 fusion.3
  82.6 0.5 fusion.4
  83.1 136.3 %all-gather.9.cloned.1.call-done = bf16[6144,2304]{0,1:T(8,128)(2,1)} async-done(((bf16[768,2304]{0,1:T(8,128)(2,1)}), bf16[6144,2304]{0,1:T(8,128)(2,1)}) %all-gather.9.cloned.1.call-update) | async-done | bytes 28311568 | tf_op jit(solution)/shard_map/all_gather | solution.py:86
  219.4 12.7 %fusion.43 = f32[128,2304]{0,1:T(8,128)S(1)} fusion(bf16[128,6144]{1,0:T(8,128)(2,1)S(1)} %fusion.4, bf16[6144,2304]{0,1:T(8,128)(2,1)} %all-gather.9.cloned.1.call-done), kind=kOutput, calls=%fused_computation.75 | convolution fusion | flops 3623878656 | bytes 31064064 | tf_op jit(solution)/shard_map/dot_general | solution.py:84
  232.3 0.3 fusion.38
  232.9 1.4 multiply_reduce_fusion.1
  234.5 0.9 fusion.11
  235.5 1.0 multiply_reduce_fusion.3
  236.5 1.6 fusion.30
  238.2 1.3 fusion.21
  239.6 0.9 pad_maximum_fusion
  240.5 1.2 copy.59
  241.8 3.6 %all-to-all-start = ((bf16[128,8,768]{2,0,1:T(8,128)(2,1)}), bf16[128,8,768]{2,0,1:T(8,128)(2,1)S(1)}, u32[]{:S(2)}, u32[]{:S(2)}) async-start(bf16[128,8,768]{2,0,1:T(8,128)(2,1)} %bitcast.92), calls=%async_computation | async-start | bytes 3145728 | tf_op jit(solution)/shard_map/all_to_all | solution.py:102
  246.0 60.2 %psum.15 = f32[]{:T(128)} all-reduce(f32[]{:T(128)} %get-tuple-element.10), channel_id=1, replica_groups=mesh['dp'=8,'mp'=4] {'dp','mp'}, use_global_device_ids=true, to_apply=%region_15.16 | all-reduce | flops 1 | bytes 8 | tf_op jit(solution)/shard_map/psum | solution.py:97
  306.9 8.4 %fusion.44 = f32[768,3,768]{2,0,1:T(8,128)} fusion(bf16[1024,768,1]{1,0,2:T(8,128)(2,1)S(1)} %bitcast.107, bf16[3,768,1024]{2,1,0:T(8,128)(2,1)} %bitcast.108), kind=kOutput, calls=%fused_computation.76 | convolution fusion | flops 3623878656 | bytes 13369344 | tf_op jit(solution)/shard_map/dot_general | solution.py:104
  (41 shorter events, 1.4 us)
Async XLA Ops:
  7.2 32.7 %copy-start = (bf16[128,588]{0,1:T(8,128)(2,1)S(1)}, bf16[128,588]{0,1:T(8,128)(2,1)}, u32[]{:S(2)}) copy-start(bf16[128,588]{0,1:T(8,128)(2,1)} %param.6) | copy-start | bytes 451588
  7.2 32.7 %all-gather.5.cloned.1.call-start = ((), (), s32[]{:S(2)}) async-start(), calls=%async_computation.1 | async-start | bytes 2211840 | tf_op jit(solution)/shard_map/all_gather | solution.py:77
  7.9 72.3 %all-gather.7.cloned.1.call-start = ((), (), s32[]{:S(2)}) async-start(), calls=%async_computation.2 | async-start | bytes 1966080 | tf_op jit(solution)/shard_map/all_gather | solution.py:80
  43.0 176.4 %all-gather.9.cloned.1.call-start = ((), (), s32[]{:S(2)}) async-start(), calls=%async_computation.3 | async-start | bytes 31850496 | tf_op jit(solution)/shard_map/all_gather | solution.py:86
  49.1 0.7 copy-start.6
  49.1 16.3 %copy-start.4 = (bf16[128,768]{1,0:T(8,128)(2,1)S(1)}, bf16[128,768]{1,0:T(8,128)(2,1)}, u32[]{:S(2)}) copy-start(bf16[128,768]{1,0:T(8,128)(2,1)} %param.11) | copy-start | bytes 589828
  49.1 16.5 %copy-start.5 = (s32[128]{0:T(128)S(1)}, s32[128]{0:T(128)}, u32[]{:S(2)}) copy-start(s32[128]{0:T(128)} %param.10) | copy-start | bytes 1540
  49.1 257.8 %all-gather.11.cloned.1.call-start = ((), (), s32[]{:S(2)}) async-start(), calls=%async_computation.4 | async-start | bytes 5308416 | tf_op jit(solution)/shard_map/all_gather | solution.py:106
  80.2 1.9 copy-start.1
  234.5 2.0 copy-start.3
  238.1 1.4 copy-start.2
  241.8 65.1 %all-to-all-start = ((bf16[128,8,768]{2,0,1:T(8,128)(2,1)}), bf16[128,8,768]{2,0,1:T(8,128)(2,1)S(1)}, u32[]{:S(2)}, u32[]{:S(2)}) async-start(bf16[128,8,768]{2,0,1:T(8,128)(2,1)} %bitcast.92), calls=%async_computation | async-start | bytes 3145728 | tf_op jit(solution)/shard_map/all_to_all | solution.py:102
Sparse Core Ops, SparseCore 0:
  9.9 29.9 all-gather.4
  43.1 37.0 all-gather.6
  82.7 136.7 all-gather.8
  240.6 52.0 all-gather.10
where the time goes:
time: 324 us; the launch traced here: 323 us
  waiting for transfers between devices  183 us (56%)
  blocking collectives  74.6 us (23%)
  matrix products  28.5 us (9%)
  between operations  17.1 us (5%)
  local copies, waits for them, and re-layouts  8.09 us (2%)
  other arithmetic  7.53 us (2%)
  starting transfers between devices  3.74 us (1%)
    all_gather x1, waiting for transfers between devices, local(): lax.all_gather(flat_weight, 'dp', axis=0, tiled=True)  136 us
    psum x1, blocking collectives, local(): loss_value = lax.psum(squared_sum, ('dp', 'mp')) / (2.0 * patch_total)  60.2 us
    all_gather x1, waiting for transfers between devices, local(): lax.all_gather(embed_weight, 'dp', axis=0, tiled=True)  31.9 us
    all_gather x1, waiting for transfers between devices, local(): embedded = lax.all_gather(own_features, 'mp', axis=1, tiled=True)  14.5 us
    psum x1, blocking collectives, local(): patch_total = lax.psum(local_total, 'dp')  14.4 us
    dot_general x1, matrix products, local(): jnp.dot(section, lax.all_gather(flat_weight, 'dp', axis=0, tiled=True), p...  12.7 us
    dot_general x1, matrix products, local(): lax.dot_general(section, lax.all_gather(grad_rows, 'dp', axis=0, tiled=Tr...  8.4 us
    unnamed x16, local copies, waits for them, and re-layouts  6.84 us
  transfers between devices with their start and end apart: 5, of which 3 were waited for; matrix products, arithmetic and copies ran while one was open for 3% of the time, Pallas kernels for 0%

commit v1 on v0

--- a/solution.py
+++ b/solution.py
@@ -1,11 +1,358 @@
+import functools
 import math
 
 import jax
 import jax.numpy as jnp
 from jax import lax
+from jax.experimental import pallas as pl
+from jax.experimental.pallas import tpu as pltpu
 from jax.sharding import PartitionSpec as P
 
 HD = 128
+MESH = pl.DeviceIdType.MESH
+VMEM_BYTES = 62 * 1024 * 1024
+
+
+def remote(src, dst, send_sem, recv_sem, device_id):
+    return pltpu.make_async_remote_copy(
+        src_ref=src, dst_ref=dst, send_sem=send_sem, recv_sem=recv_sem,
+        device_id=device_id, device_id_type=MESH,
+    )
+
+
+def greet(n, n_mp, d, m):
+    barrier = pltpu.get_barrier_semaphore()
+    for i in range(1, n):
+        pl.semaphore_signal(barrier, inc=1, device_id={"dp": lax.rem(d + i, n)}, device_id_type=MESH)
+    for i in range(1, n_mp):
+        pl.semaphore_signal(barrier, inc=1, device_id={"mp": lax.rem(m + i, n_mp)}, device_id_type=MESH)
+    pl.semaphore_wait(barrier, n - 1 + n_mp - 1)
+
+
+def project_kernel(
+    n, n_mp,
+    patches, embed, weight_hbm, counts,
+    normed, raw, total,
+    pall, zbuf, eblk, wbuf, stats, cbuf, pbuf, pin, sbuf, rbuf,
+    w_sem, cs, cr, ps, pr, fs, fr, zs, zr, es, er, ss, sr, bs, br, qs, qr, loc_sem,
+):
+    d, m = lax.axis_index("dp"), lax.axis_index("mp")
+    core, chip = lax.rem(d, 2), d // 2
+    partner = d + 1 - 2 * core
+    nc, per = n // 2, n // n_mp
+    rows = patches.shape[0]
+    tile = weight_hbm.shape[2]
+
+    load = pltpu.make_async_copy(weight_hbm, wbuf, w_sem)
+    load.start()
+    greet(n, n_mp, d, m)
+
+    def peer(i):
+        return 2 * lax.rem(chip + i, nc) + core
+
+    def source(i):
+        return 2 * lax.rem(chip + nc - i, nc) + core
+
+    def far(i):
+        return lax.rem(d + i, n)
+
+    def z_copy(i):
+        return remote(embed, zbuf.at[i], zs.at[i], zr.at[i], {"mp": lax.rem(m + i, n_mp)})
+
+    for i in range(1, n_mp):
+        z_copy(i).start()
+
+    def c_copy(i):
+        return remote(counts, cbuf.at[i], cs.at[i], cr.at[i], {"dp": far(i)})
+
+    def p_copy(i):
+        return remote(patches, pall.at[d], ps.at[i], pr.at[i], {"dp": peer(i)})
+
+    def p_own():
+        return remote(patches, pall.at[d], ps.at[0], pr.at[0], {"dp": partner})
+
+    def f_copy(i):
+        return remote(pall.at[source(i)], pall.at[source(i)], fs.at[i], fr.at[i], {"dp": partner})
+
+    def e_target(i):
+        return lax.rem(m + n_mp - i, n_mp) * per + d // n_mp
+
+    def e_copy(i, src):
+        return remote(src, eblk.at[lax.rem(d, n_mp)], es.at[i], er.at[lax.rem(d, n_mp)], {"dp": e_target(i)})
+
+    def e_local(i, src):
+        return pltpu.make_async_copy(src, eblk.at[lax.rem(d, n_mp)], loc_sem)
+
+    def e_start(i, src):
+        @pl.when(e_target(i) != d)
+        def _():
+            e_copy(i, src).start()
+
+        @pl.when(e_target(i) == d)
+        def _():
+            e_local(i, src).start()
+            e_local(i, src).wait()
+
+    p_own().start()
+    for i in range(1, nc):
+        p_copy(i).start()
+    for i in range(1, n):
+        c_copy(i).start()
+    e_start(0, embed)
+    pall[d] = patches[...]
+    for i in range(1, nc):
+        p_copy(i).wait_recv()
+        f_copy(i).start()
+    for i in range(1, n_mp):
+        z_copy(i).wait_recv()
+        e_start(i, zbuf.at[i])
+    sum_counts = counts[...]
+    for i in range(1, n):
+        c_copy(i).wait_recv()
+        sum_counts = sum_counts + cbuf[i]
+    total[...] = sum_counts
+    p_own().wait_recv()
+    for i in range(1, nc):
+        f_copy(i).wait_recv()
+    for q in range(n_mp):
+        origin = lax.rem(d, per) * n_mp + q
+
+        @pl.when(origin != d)
+        def _():
+            remote(eblk.at[q], eblk.at[q], es.at[q], er.at[q], {"dp": partner}).wait_recv()
+
+    width = eblk.shape[0] * eblk.shape[1]
+    feature_total = width * n
+    lane = lax.broadcasted_iota(jnp.int32, (rows, 128), 1)
+
+    def embed_block(b, carry):
+        block = pall[b]
+        parts = jnp.concatenate(
+            [eblk[q] for q in range(n_mp)], axis=0
+        )
+        value = lax.dot_general(
+            block, parts, (((1,), (1,)), ((), ())), preferred_element_type=jnp.float32
+        ).astype(jnp.bfloat16)
+        normed[b] = value
+        value = value.astype(jnp.float32)
+        mean = jnp.sum(value, axis=-1, keepdims=True) * (1.0 / width)
+        center = value - mean
+        square = jnp.sum(center * center, axis=-1, keepdims=True)
+        both = jnp.where(lane == 0, mean, jnp.where(lane == 1, square, 0.0))
+        stats[0, b] = both.T[:8]
+        return carry
+
+    lax.fori_loop(0, n, embed_block, 0)
+
+    def s_copy(i):
+        return remote(stats.at[0], stats.at[i], ss.at[i], sr.at[i], {"dp": far(i)})
+
+    for i in range(1, n):
+        s_copy(i).start()
+    for i in range(1, n):
+        s_copy(i).wait_recv()
+
+    load.wait()
+
+    def norm_block(b, carry):
+        mean = stats[0, b, 0:1, :]
+        for i in range(1, n):
+            mean = mean + stats[i, b, 0:1, :]
+        mean = mean * (1.0 / n)
+        square = jnp.zeros_like(mean)
+        for i in range(n):
+            gap = stats[i, b, 0:1, :] - mean
+            square = square + stats[i, b, 1:2, :] + width * (gap * gap)
+        scale = lax.rsqrt(square * (1.0 / feature_total) + 1e-06)
+        row = lax.broadcasted_iota(jnp.int32, (128, rows), 0)
+        both = jnp.where(row == 0, mean, jnp.where(row == 1, scale, 0.0)).T
+        value = normed[b].astype(jnp.float32)
+        normed[b] = ((value - both[:, 0:1]) * both[:, 1:2]).astype(jnp.bfloat16)
+        return carry
+
+    lax.fori_loop(0, n, norm_block, 0)
+
+    def b_copy(i):
+        return remote(pbuf.at[i], pin.at[i], bs.at[i], br.at[i], {"dp": partner})
+
+    def q_copy(i):
+        return remote(sbuf.at[i], rbuf.at[i], qs.at[i], qr.at[i], {"dp": peer(i)})
+
+    def other_part(k, carry):
+        i = lax.rem(k + 1, nc)
+        block = normed[2 * lax.rem(chip + i, nc) + 1 - core]
+        for s in range(3):
+            pbuf[i, :, s * tile:(s + 1) * tile] = jnp.dot(
+                block, wbuf[s], preferred_element_type=jnp.float32
+            ).astype(jnp.bfloat16)
+        b_copy(i).start()
+        return carry
+
+    lax.fori_loop(0, nc, other_part, 0)
+
+    def own_part(i, carry):
+        block = normed[peer(i)]
+        b_copy(i).wait_recv()
+        for s in range(3):
+            cols = slice(s * tile, (s + 1) * tile)
+            sbuf[i, :, cols] = (
+                jnp.dot(block, wbuf[s], preferred_element_type=jnp.float32)
+                + pin[i, :, cols].astype(jnp.float32)
+            ).astype(jnp.bfloat16)
+        q_copy(i).start()
+        return carry
+
+    lax.fori_loop(1, nc, own_part, 0)
+    block = normed[d]
+    b_copy(0).wait_recv()
+    for s in range(3):
+        cols = slice(s * tile, (s + 1) * tile)
+        raw[:, cols] = jnp.dot(block, wbuf[s], preferred_element_type=jnp.float32) + pin[
+            0, :, cols
+        ].astype(jnp.float32)
+
+    def take(i, carry):
+        q_copy(i).wait_recv()
+        raw[...] += rbuf[i].astype(jnp.float32)
+        return carry
+
+    lax.fori_loop(1, nc, take, 0)
+
+    p_own().wait_send()
+    for i in range(1, n_mp):
+        z_copy(i).wait_send()
+    for i in range(n_mp):
+        @pl.when(e_target(i) != d)
+        def _():
+            e_copy(i, embed).wait_send()
+    for i in range(1, nc):
+        p_copy(i).wait_send()
+        f_copy(i).wait_send()
+        q_copy(i).wait_send()
+    for i in range(nc):
+        b_copy(i).wait_send()
+    for i in range(1, n):
+        c_copy(i).wait_send()
+        s_copy(i).wait_send()
+
+
+def project(patches, embed, weight, counts, n, n_mp):
+    rows, width = patches.shape
+    pieces = embed.shape[0]
+    features, columns = weight.shape[1], 3 * weight.shape[2]
+    nc = n // 2
+    dma = lambda k: pltpu.SemaphoreType.DMA((k,))
+    vmem = pl.BlockSpec(memory_space=pltpu.VMEM)
+    bf16, f32 = jnp.bfloat16, jnp.float32
+    return pl.pallas_call(
+        functools.partial(project_kernel, n, n_mp),
+        out_shape=(
+            jax.ShapeDtypeStruct((n, rows, features), bf16),
+            jax.ShapeDtypeStruct((rows, columns), f32),
+            jax.ShapeDtypeStruct((8, 128), f32),
+        ),
+        in_specs=[vmem, vmem, pl.BlockSpec(memory_space=pl.ANY), vmem],
+        out_specs=(vmem, vmem, vmem),
+        scratch_shapes=[
+            pltpu.VMEM((n, rows, width), bf16),
+            pltpu.VMEM((n_mp, pieces, width), bf16),
+            pltpu.VMEM((n_mp, pieces, width), bf16),
+            pltpu.VMEM(weight.shape, bf16),
+            pltpu.VMEM((n, n, 8, rows), f32),
+            pltpu.VMEM((n, 8, 128), f32),
+            pltpu.VMEM((nc, rows, columns), bf16),
+            pltpu.VMEM((nc, rows, columns), bf16),
+            pltpu.VMEM((nc, rows, columns), bf16),
+            pltpu.VMEM((nc, rows, columns), bf16),
+            pltpu.SemaphoreType.DMA,
+            dma(n), dma(n), dma(nc), dma(nc), dma(nc), dma(nc), dma(n_mp), dma(n_mp),
+            dma(n_mp), dma(n_mp), dma(n), dma(n), dma(nc), dma(nc), dma(nc), dma(nc),
+            pltpu.SemaphoreType.DMA,
+        ],
+        compiler_params=pltpu.CompilerParams(
+            collective_id=0, has_side_effects=True, vmem_limit_bytes=VMEM_BYTES
+        ),
+    )(patches, embed, weight, counts)
+
+
+def spread_kernel(n, n_mp, grads, squares, gathered, loss, zsq, psq, mine, ps, pr, fs, fr, zs, zr, cs, cr, loc_sem):
+    d, m = lax.axis_index("dp"), lax.axis_index("mp")
+    core, chip = lax.rem(d, 2), d // 2
+    partner = d + 1 - 2 * core
+    nc = n // 2
+    greet(n, n_mp, d, m)
+
+    def g_copy(i):
+        return remote(grads, gathered.at[d], ps.at[i], pr.at[i], {"dp": 2 * lax.rem(chip + i, nc) + core})
+
+    def g_own():
+        return remote(grads, gathered.at[d], ps.at[0], pr.at[0], {"dp": partner})
+
+    def f_copy(i):
+        source = 2 * lax.rem(chip + nc - i, nc) + core
+        return remote(gathered.at[source], gathered.at[source], fs.at[i], fr.at[i], {"dp": partner})
+
+    def z_copy(i):
+        return remote(squares, zsq.at[i], zs.at[i], zr.at[i], {"mp": lax.rem(m + i, n_mp)})
+
+    def c_copy(i):
+        return remote(mine, psq.at[i], cs.at[i], cr.at[i], {"dp": lax.rem(d + i, n)})
+
+    for i in range(1, n_mp):
+        z_copy(i).start()
+    for i in range(1, nc):
+        g_copy(i).start()
+    g_own().start()
+    own = pltpu.make_async_copy(grads, gathered.at[d], loc_sem)
+    own.start()
+    value = squares[...]
+    for i in range(1, n_mp):
+        z_copy(i).wait_recv()
+        value = value + zsq[i]
+    mine[...] = value
+    for i in range(1, n):
+        c_copy(i).start()
+    for i in range(1, nc):
+        g_copy(i).wait_recv()
+        f_copy(i).start()
+    for i in range(1, n):
+        c_copy(i).wait_recv()
+        value = value + psq[i]
+    loss[...] = value
+    g_own().wait()
+    own.wait()
+    for i in range(1, n_mp):
+        z_copy(i).wait_send()
+    for i in range(1, nc):
+        g_copy(i).wait_send()
+        f_copy(i).wait()
+    for i in range(1, n):
+        c_copy(i).wait_send()
+
+
+def spread(grads, squares, n, n_mp):
+    nc = n // 2
+    dma = lambda k: pltpu.SemaphoreType.DMA((k,))
+    vmem = pl.BlockSpec(memory_space=pltpu.VMEM)
+    return pl.pallas_call(
+        functools.partial(spread_kernel, n, n_mp),
+        out_shape=(
+            jax.ShapeDtypeStruct((n,) + grads.shape, grads.dtype),
+            jax.ShapeDtypeStruct((8, 128), jnp.float32),
+        ),
+        in_specs=[vmem, vmem],
+        out_specs=(vmem, vmem),
+        scratch_shapes=[
+            pltpu.VMEM((n_mp, 8, 128), jnp.float32),
+            pltpu.VMEM((n, 8, 128), jnp.float32),
+            pltpu.VMEM((8, 128), jnp.float32),
+            dma(nc), dma(nc), dma(nc), dma(nc), dma(n_mp), dma(n_mp), dma(n), dma(n),
+            pltpu.SemaphoreType.DMA,
+        ],
+        compiler_params=pltpu.CompilerParams(
+            collective_id=1, has_side_effects=True, vmem_limit_bytes=VMEM_BYTES
+        ),
+    )(grads, squares)
 
 
 def layer_norm(values):
@@ -67,25 +414,13 @@
     return jnp.stack([query_grad, key_grad, value_grad], axis=1)
 
 
-def local(patches, embed_weight, project_weight, patch_counts, segment_ids, targets):
-    local_total = jnp.sum(patch_counts).astype(jnp.float32)
-    patch_total = lax.psum(local_total, "dp")
+def local(n, n_mp, patches, embed_weight, project_weight, patch_counts, segment_ids, targets):
+    counts = jnp.broadcast_to(jnp.sum(patch_counts).astype(jnp.float32), (8, 128))
     row_total = patches.shape[0]
-    own_features = jnp.einsum(
-        "rp,cp->rc",
-        patches,
-        lax.all_gather(embed_weight, "dp", axis=0, tiled=True),
-        preferred_element_type=jnp.float32,
-    ).astype(jnp.bfloat16)
-    embedded = lax.all_gather(own_features, "mp", axis=1, tiled=True)
-    normed = layer_norm(embedded.astype(jnp.float32)).astype(jnp.bfloat16)
-    flat_weight = project_weight.reshape(project_weight.shape[0], -1)
-    section = normed
-    projected = jnp.dot(
-        section,
-        lax.all_gather(flat_weight, "dp", axis=0, tiled=True),
-        preferred_element_type=jnp.float32,
-    )
+    normed, projected, total = project(
+        patches, embed_weight, jnp.transpose(project_weight, (1, 0, 2)), counts, n, n_mp
+    )
+    patch_total = total[0, 0]
     head_dev = project_weight.shape[2] // HD
     projected = projected.reshape(row_total, 3, head_dev, HD)
     query_raw = projected[:, 0]
@@ -94,16 +429,16 @@
     query_normed, key_normed, weights, error_rows, squared_sum = attend_block(
         query_raw, key_raw, value_rows, segment_ids, targets
     )
-    loss_value = lax.psum(squared_sum, ("dp", "mp")) / (2.0 * patch_total)
     grad_rows = attend_back(
         query_raw, key_raw, query_normed, key_normed, value_rows, weights, error_rows, patch_total
     )
-    grad_rows = grad_rows.reshape(row_total, -1)
-    normed_blocks = lax.all_to_all(normed, "dp", split_axis=1, concat_axis=0, tiled=True)
-    section = normed_blocks
+    gathered, squares = spread(
+        grad_rows.reshape(row_total, -1), jnp.broadcast_to(squared_sum, (8, 128)), n, n_mp
+    )
+    loss_value = squares[0, 0] / (2.0 * patch_total)
     weight_grad = lax.dot_general(
-        section,
-        lax.all_gather(grad_rows, "dp", axis=0, tiled=True),
+        normed.reshape(-1, normed.shape[2]),
+        gathered.reshape(-1, gathered.shape[2]),
         (((0,), (0,)), ((), ())),
         preferred_element_type=jnp.float32,
     )
@@ -120,4 +455,5 @@
         P("dp", "mp"),
     )
     out_specs = (P("dp", None, "mp"), P())
-    return jax.shard_map(local, mesh=mesh, in_specs=in_specs, out_specs=out_specs, check_vma=False)
+    return jax.shard_map(
+        functools.partial(local, mesh.shape["dp"], mesh.shape["mp"]), mesh=mesh, in_specs=in_specs, out_specs=out_specs, check_vma=False)

time: 324 us -> 156 us (0.48)
  waiting for transfers between devices: 183 us -> 0 us
  Pallas kernels: 0 us -> 121 us
  blocking collectives: 74.6 us -> 0 us
  matrix products: 28.5 us -> 9.95 us
  between operations: 17.1 us -> 3.9 us
  local copies, waits for them, and re-layouts: 8.09 us -> 16.5 us
  starting transfers between devices: 3.74 us -> 0 us
    all_gather x4 -> x0, waiting for transfers between devices: 183 us -> none  [the longest x1 136 us: local(): lax.all_gather(flat_weight, 'dp', axis=0, tiled=True)]
    pallas_call x0 -> x2, Pallas kernels: none -> 121 us  [the longest x1 80.8 us: project(): pl.pallas_call(functools.partial(project_kernel, n, n_mp), out_shape=(jax...]
    psum x2 -> x0, blocking collectives: 74.6 us -> none  [the longest x1 60.2 us: local(): loss_value = lax.psum(squared_sum, ('dp', 'mp')) / (2.0 * patch_total)]
    dot_general x3 -> x1, matrix products: 24.2 us -> 8.33 us  [local(): lax.dot_general(normed.reshape(-1, normed.shape[2]), gathered.reshape(-1,...]
    dot_general x0 -> x1, local copies, waits for them, and re-layouts: none -> 6.83 us  [local(): lax.dot_general(normed.reshape(-1, normed.shape[2]), gathered.reshape(-1,...]
    unnamed x16 -> x4, local copies, waits for them, and re-layouts: 6.84 us -> 2.81 us
    all_to_all x1 -> x0, starting transfers between devices: 3.58 us -> none  [local(): lax.all_to_all(normed, 'dp', split_axis=1, concat_axis=0, tiled=True)]
  transfers between devices with their start and end apart: 5 -> 0, of which waited for: 3 -> 0; matrix products, arithmetic and copies ran while one was open for 3% -> 0% of each run, Pallas kernels for 0% -> 0%
where the time goes in v1:
time: 156 us
  Pallas kernels  121 us (78%)
  local copies, waits for them, and re-layouts  16.5 us (11%)
  matrix products  9.95 us (6%)
  other arithmetic  4.75 us (3%)
  between operations  3.9 us (2%)
    pallas_call x1, Pallas kernels, project(): pl.pallas_call(functools.partial(project_kernel, n, n_mp), out_shape=(jax...  80.8 us
    pallas_call x1, Pallas kernels, spread(): pl.pallas_call(functools.partial(spread_kernel, n, n_mp), out_shape=(jax....  40 us
    dot_general x1, matrix products, local(): lax.dot_general(normed.reshape(-1, normed.shape[2]), gathered.reshape(-1,...  8.33 us
    dot_general x1, local copies, waits for them, and re-layouts, local(): lax.dot_general(normed.reshape(-1, normed.shape[2]), gathered.reshape(-1,...  6.83 us

profile of v1, /device:TPU:0, one launch (start us, length us, event | category | flops | bytes accessed | tf_op | source)
XLA Modules:
  0.0 155.9 jit_solution(4984988068030524795)
XLA Ops:
  0.6 1.3 reduce_sum.105
  2.6 0.7 broadcast_compare_fusion
  3.2 0.6 broadcast_in_dim.70.counts
  3.8 0.8 compare_and_fusion
  4.6 1.7 %copy.25.patches = bf16[128,588]{1,0:T(8,128)(2,1)} copy(bf16[128,588]{0,1:T(8,128)(2,1)} %param.6) | data formatting | bytes 301056 | tf_op args[0]
  6.4 1.1 copy.30
  7.5 80.8 %shard_map.77 = (bf16[8,128,768]{2,1,0:T(8,128)(2,1)}, f32[128,2304]{1,0:T(8,128)}, f32[8,128]{1,0:T(8,128)}) custom-call(bf16[128,588]{1,0:T(8,128)(2,1)} %copy.25.patches, bf16[192,588]{1,0:T(8,128)(2,1)} %embed.1, bf16[3,768,768]{2,1,0:T(8,128)(2,1)} %bitcast.96, f32[8,128]{1,0:T(8,128)} %broadcast_in_dim.70.counts), custom_call_target="tpu_custom_call" | custom-call | tf_op jit(solution)/shard_map/pallas_call | solution.py:247
  88.3 1.2 slice.19
  90.1 1.6 %copy.26 = f32[128,2304]{0,1:T(8,128)S(1)} copy(f32[128,2304]{1,0:T(8,128)} %get-tuple-element.8) | data formatting | bytes 2359296 | tf_op jit(solution)/shard_map/pallas_call | solution.py:247
  91.9 0.3 fusion.34
  92.3 0.2 fusion.24
  92.5 1.4 multiply_reduce_fusion.1
  93.9 1.2 broadcast_in_dim.81.squares
  95.1 0.3 fusion.7
  95.4 0.3 fusion.22
  95.6 0.3 multiply_reduce_fusion.3
  95.9 0.3 fusion.26
  96.3 0.2 fusion.17
  96.5 0.1 fusion.18
  96.7 1.1 copy.36.grads
  97.8 40.0 %shard_map.78 = (bf16[8,128,2304]{2,1,0:T(8,128)(2,1)}, f32[8,128]{1,0:T(8,128)}) custom-call(bf16[128,2304]{1,0:T(8,128)(2,1)} %copy.36.grads, f32[8,128]{1,0:T(8,128)} %broadcast_in_dim.81.squares), custom_call_target="tpu_custom_call" | custom-call | tf_op jit(solution)/shard_map/pallas_call | solution.py:337
  137.8 1.2 slice.20
  139.6 6.8 %copy.37 = bf16[2304,1024]{1,0:T(8,128)(2,1)} copy(bf16[2304,1024]{0,1:T(8,128)(2,1)} %bitcast.94) | data formatting | bytes 9437184 | tf_op jit(solution)/shard_map/dot_general | solution.py:439
  146.5 8.3 %fusion.39 = f32[768,3,768]{2,0,1:T(8,128)} fusion(bf16[1024,768,1]{1,0,2:T(8,128)(2,1)S(1)} %bitcast.100, bf16[3,768,1024]{2,1,0:T(8,128)(2,1)} %bitcast.95), kind=kOutput, calls=%fused_computation.65 | convolution fusion | flops 3623878656 | bytes 13369344 | tf_op jit(solution)/shard_map/dot_general | solution.py:439
  (14 shorter events, 0.3 us)
Async XLA Ops:
  139.6 6.8 %copy-start = (bf16[8,128,768]{2,1,0:T(8,128)(2,1)S(1)}, bf16[8,128,768]{2,1,0:T(8,128)(2,1)}, u32[]{:S(2)}) copy-start(bf16[8,128,768]{2,1,0:T(8,128)(2,1)} %get-tuple-element.7) | copy-start | bytes 4718596

commit v2 on v1

--- a/solution.py
+++ b/solution.py
@@ -275,22 +275,48 @@
     )(patches, embed, weight, counts)
 
 
-def spread_kernel(n, n_mp, grads, squares, gathered, loss, zsq, psq, mine, ps, pr, fs, fr, zs, zr, cs, cr, loc_sem):
+def grid_side(nc):
+    side = math.isqrt(nc)
+    assert side * side == nc
+    return side
+
+
+def chip_at(chip, side, h, i, j):
+    a, b = chip // side, lax.rem(chip, side)
+    da, db = (j, i) if h == 0 else (i, j)
+    return lax.rem(a + da + side, side) * side + lax.rem(b + db + side, side)
+
+
+def spread_kernel(n, n_mp, chunks, grads, squares, gathered, loss, zsq, psq, mine, ps, pr, gs, gr, fs, fr, zs, zr, cs, cr, loc_sem):
     d, m = lax.axis_index("dp"), lax.axis_index("mp")
     core, chip = lax.rem(d, 2), d // 2
     partner = d + 1 - 2 * core
     nc = n // 2
+    side = grid_side(nc)
+    span = grads.shape[0] // chunks
     greet(n, n_mp, d, m)
 
-    def g_copy(i):
-        return remote(grads, gathered.at[d], ps.at[i], pr.at[i], {"dp": 2 * lax.rem(chip + i, nc) + core})
-
-    def g_own():
-        return remote(grads, gathered.at[d], ps.at[0], pr.at[0], {"dp": partner})
-
-    def f_copy(i):
-        source = 2 * lax.rem(chip + nc - i, nc) + core
-        return remote(gathered.at[source], gathered.at[source], fs.at[i], fr.at[i], {"dp": partner})
+    def part(k):
+        return pl.ds(k * span, span)
+
+    def block(k, i, j):
+        if i == 0 and j == 0:
+            return grads.at[part(k)]
+        return gathered.at[2 * chip_at(chip, side, k % 2, -i, -j) + core, part(k)]
+
+    def landing(k, i, j):
+        return gathered.at[2 * chip_at(chip, side, k % 2, -i, -j) + core, part(k)]
+
+    def first(k, i):
+        to = 2 * chip_at(chip, side, k % 2, i, 0) + core
+        return remote(block(k, 0, 0), landing(k, 0, 0), ps.at[k, i], pr.at[k, i], {"dp": to})
+
+    def second(k, i, j):
+        to = 2 * chip_at(chip, side, k % 2, 0, j) + core
+        return remote(block(k, i, 0), landing(k, i, 0), gs.at[k, i, j], gr.at[k, i, j], {"dp": to})
+
+    def across(k, i, j):
+        return remote(block(k, i, j), landing(k, i, j), fs.at[k, i, j], fr.at[k, i, j], {"dp": partner})
 
     def z_copy(i):
         return remote(squares, zsq.at[i], zs.at[i], zr.at[i], {"mp": lax.rem(m + i, n_mp)})
@@ -300,9 +326,13 @@
 
     for i in range(1, n_mp):
         z_copy(i).start()
-    for i in range(1, nc):
-        g_copy(i).start()
-    g_own().start()
+    for k in range(chunks):
+        for i in range(1, side):
+            first(k, i).start()
+    for k in range(chunks):
+        for j in range(1, side):
+            second(k, 0, j).start()
+        across(k, 0, 0).start()
     own = pltpu.make_async_copy(grads, gathered.at[d], loc_sem)
     own.start()
     value = squares[...]
@@ -312,30 +342,43 @@
     mine[...] = value
     for i in range(1, n):
         c_copy(i).start()
-    for i in range(1, nc):
-        g_copy(i).wait_recv()
-        f_copy(i).start()
+    for k in range(chunks):
+        for i in range(1, side):
+            first(k, i).wait_recv()
+            for j in range(1, side):
+                second(k, i, j).start()
+            across(k, i, 0).start()
     for i in range(1, n):
         c_copy(i).wait_recv()
         value = value + psq[i]
     loss[...] = value
-    g_own().wait()
+    for i in range(side):
+        for k in range(chunks):
+            for j in range(1, side):
+                second(k, i, j).wait_recv()
+                across(k, i, j).start()
     own.wait()
+    for k in range(chunks):
+        for i in range(side):
+            if i:
+                first(k, i).wait_send()
+            for j in range(side):
+                if j:
+                    second(k, i, j).wait_send()
+                across(k, i, j).wait()
     for i in range(1, n_mp):
         z_copy(i).wait_send()
-    for i in range(1, nc):
-        g_copy(i).wait_send()
-        f_copy(i).wait()
     for i in range(1, n):
         c_copy(i).wait_send()
 
 
 def spread(grads, squares, n, n_mp):
-    nc = n // 2
-    dma = lambda k: pltpu.SemaphoreType.DMA((k,))
+    chunks = 4
+    side = grid_side(n // 2)
+    dma = lambda *k: pltpu.SemaphoreType.DMA(k)
     vmem = pl.BlockSpec(memory_space=pltpu.VMEM)
     return pl.pallas_call(
-        functools.partial(spread_kernel, n, n_mp),
+        functools.partial(spread_kernel, n, n_mp, chunks),
         out_shape=(
             jax.ShapeDtypeStruct((n,) + grads.shape, grads.dtype),
             jax.ShapeDtypeStruct((8, 128), jnp.float32),
@@ -346,13 +389,38 @@
             pltpu.VMEM((n_mp, 8, 128), jnp.float32),
             pltpu.VMEM((n, 8, 128), jnp.float32),
             pltpu.VMEM((8, 128), jnp.float32),
-            dma(nc), dma(nc), dma(nc), dma(nc), dma(n_mp), dma(n_mp), dma(n), dma(n),
+            dma(chunks, side), dma(chunks, side),
+            dma(chunks, side, side), dma(chunks, side, side),
+            dma(chunks, side, side), dma(chunks, side, side),
+            dma(n_mp), dma(n_mp), dma(n), dma(n),
             pltpu.SemaphoreType.DMA,
         ],
         compiler_params=pltpu.CompilerParams(
             collective_id=1, has_side_effects=True, vmem_limit_bytes=VMEM_BYTES
         ),
     )(grads, squares)
+
+
+def weight_grad_kernel(left, right, out):
+    out[0] = lax.dot_general(
+        left[...], right[...], (((0,), (0,)), ((), ())), preferred_element_type=jnp.float32
+    )
+
+
+def weight_grad_of(normed, grads):
+    rows, features = normed.shape
+    tile = grads.shape[1] // 3
+    width = 256 if features % 256 == 0 else features
+    return pl.pallas_call(
+        weight_grad_kernel,
+        grid=(3, features // width),
+        out_shape=jax.ShapeDtypeStruct((3, features, tile), jnp.float32),
+        in_specs=[
+            pl.BlockSpec((rows, width), lambda s, f: (0, f)),
+            pl.BlockSpec((rows, tile), lambda s, f: (0, s)),
+        ],
+        out_specs=pl.BlockSpec((1, width, tile), lambda s, f: (s, f, 0)),
+    )(normed, grads)
 
 
 def layer_norm(values):
@@ -436,13 +504,10 @@
         grad_rows.reshape(row_total, -1), jnp.broadcast_to(squared_sum, (8, 128)), n, n_mp
     )
     loss_value = squares[0, 0] / (2.0 * patch_total)
-    weight_grad = lax.dot_general(
-        normed.reshape(-1, normed.shape[2]),
-        gathered.reshape(-1, gathered.shape[2]),
-        (((0,), (0,)), ((), ())),
-        preferred_element_type=jnp.float32,
-    )
-    return (weight_grad.reshape(weight_grad.shape[0], 3, -1), loss_value)
+    weight_grad = weight_grad_of(
+        normed.reshape(-1, normed.shape[2]), gathered.reshape(-1, gathered.shape[2])
+    )
+    return (jnp.transpose(weight_grad, (1, 0, 2)), loss_value)
 
 
 def solution(mesh):

time: 156 us -> 147 us (0.942)
  matrix products: 9.95 us -> 1.62 us
  local copies, waits for them, and re-layouts: 16.5 us -> 9.69 us
  Pallas kernels: 121 us -> 126 us
    dot_general x1 -> x0, matrix products: 8.33 us -> none  [local(): lax.dot_general(normed.reshape(-1, normed.shape[2]), gathered.reshape(-1,...]
    dot_general x1 -> x0, local copies, waits for them, and re-layouts: 6.83 us -> none  [local(): lax.dot_general(normed.reshape(-1, normed.shape[2]), gathered.reshape(-1,...]
    pallas_call x1 -> x2, Pallas kernels: 40 us -> 45.4 us  [the longest x1 33.7 us: spread(): pl.pallas_call(functools.partial(spread_kernel, n, n_mp, chunks), out_sha...]
where the time goes in v2:
time: 147 us; the launch traced here: 146 us
  Pallas kernels  126 us (86%)
  local copies, waits for them, and re-layouts  9.69 us (7%)
  other arithmetic  4.75 us (3%)
  between operations  3.89 us (3%)
  matrix products  1.62 us (1%)
    pallas_call x1, Pallas kernels, project(): pl.pallas_call(functools.partial(project_kernel, n, n_mp), out_shape=(jax...  80.8 us
    pallas_call x1, Pallas kernels, spread(): pl.pallas_call(functools.partial(spread_kernel, n, n_mp, chunks), out_sha...  33.7 us
    pallas_call x1, Pallas kernels, weight_grad_of(): pl.pallas_call(weight_grad_kernel, grid=(3, features // width), out_shape...  11.6 us

profile of v2, /device:TPU:0, one launch (start us, length us, event | category | flops | bytes accessed | tf_op | source)
XLA Modules:
  0.0 146.1 jit_solution(17719269231531189340)
XLA Ops:
  0.6 1.3 reduce_sum.105
  2.6 0.7 broadcast_compare_fusion
  3.2 0.6 broadcast_in_dim.70.counts
  3.8 0.8 compare_and_fusion
  4.6 1.7 %copy.23.patches = bf16[128,588]{1,0:T(8,128)(2,1)} copy(bf16[128,588]{0,1:T(8,128)(2,1)} %param.6) | data formatting | bytes 301056 | tf_op args[0]
  6.4 1.1 copy.28
  7.5 80.8 %shard_map.77 = (bf16[8,128,768]{2,1,0:T(8,128)(2,1)}, f32[128,2304]{1,0:T(8,128)}, f32[8,128]{1,0:T(8,128)}) custom-call(bf16[128,588]{1,0:T(8,128)(2,1)} %copy.23.patches, bf16[192,588]{1,0:T(8,128)(2,1)} %embed.1, bf16[3,768,768]{2,1,0:T(8,128)(2,1)} %bitcast.90, f32[8,128]{1,0:T(8,128)} %broadcast_in_dim.70.counts), custom_call_target="tpu_custom_call" | custom-call | tf_op jit(solution)/shard_map/pallas_call | solution.py:247
  88.2 1.2 slice.19
  90.1 1.6 %copy.24 = f32[128,2304]{0,1:T(8,128)S(1)} copy(f32[128,2304]{1,0:T(8,128)} %get-tuple-element.8) | data formatting | bytes 2359296 | tf_op jit(solution)/shard_map/pallas_call | solution.py:247
  91.8 0.1 multiply_reduce_fusion.4
  91.9 0.3 fusion.34
  92.3 0.2 fusion.24
  92.5 1.4 multiply_reduce_fusion.1
  93.8 1.2 broadcast_in_dim.81.squares
  95.1 0.3 fusion.7
  95.3 0.3 fusion.22
  95.6 0.3 multiply_reduce_fusion.3
  95.9 0.3 fusion.26
  96.3 0.2 fusion.17
  96.5 0.1 fusion.18
  96.7 1.1 copy.34.grads
  97.8 33.7 %shard_map.78 = (bf16[8,128,2304]{2,1,0:T(8,128)(2,1)}, f32[8,128]{1,0:T(8,128)}) custom-call(bf16[128,2304]{1,0:T(8,128)(2,1)} %copy.34.grads, f32[8,128]{1,0:T(8,128)} %broadcast_in_dim.81.squares), custom_call_target="tpu_custom_call" | custom-call | tf_op jit(solution)/shard_map/pallas_call | solution.py:380
  131.5 1.2 slice.20
  133.4 11.6 %shard_map.79 = f32[3,768,768]{2,1,0:T(8,128)} custom-call(bf16[1024,768]{1,0:T(8,128)(2,1)} %bitcast.94, bf16[1024,2304]{1,0:T(8,128)(2,1)} %bitcast.89), custom_call_target="tpu_custom_call" | custom-call | tf_op jit(solution)/shard_map/pallas_call | solution.py:414
  (11 shorter events, 0.2 us)

commit v3 on v2

--- a/solution.py
+++ b/solution.py
@@ -32,8 +32,8 @@
 def project_kernel(
     n, n_mp,
     patches, embed, weight_hbm, counts,
-    normed, raw, total,
-    pall, zbuf, eblk, wbuf, stats, cbuf, pbuf, pin, sbuf, rbuf,
+    normed_t, raw, total,
+    normed, pall, zbuf, eblk, wbuf, stats, cbuf, pbuf, pin, sbuf, rbuf,
     w_sem, cs, cr, ps, pr, fs, fr, zs, zr, es, er, ss, sr, bs, br, qs, qr, loc_sem,
 ):
     d, m = lax.axis_index("dp"), lax.axis_index("mp")
@@ -211,6 +211,9 @@
             0, :, cols
         ].astype(jnp.float32)
 
+    for b in range(n):
+        normed_t[:, b * rows:(b + 1) * rows] = normed[b].T
+
     def take(i, carry):
         q_copy(i).wait_recv()
         raw[...] += rbuf[i].astype(jnp.float32)
@@ -247,13 +250,14 @@
     return pl.pallas_call(
         functools.partial(project_kernel, n, n_mp),
         out_shape=(
-            jax.ShapeDtypeStruct((n, rows, features), bf16),
+            jax.ShapeDtypeStruct((features, n * rows), bf16),
             jax.ShapeDtypeStruct((rows, columns), f32),
             jax.ShapeDtypeStruct((8, 128), f32),
         ),
         in_specs=[vmem, vmem, pl.BlockSpec(memory_space=pl.ANY), vmem],
         out_specs=(vmem, vmem, vmem),
         scratch_shapes=[
+            pltpu.VMEM((n, rows, features), bf16),
             pltpu.VMEM((n, rows, width), bf16),
             pltpu.VMEM((n_mp, pieces, width), bf16),
             pltpu.VMEM((n_mp, pieces, width), bf16),
@@ -402,13 +406,11 @@
 
 
 def weight_grad_kernel(left, right, out):
-    out[0] = lax.dot_general(
-        left[...], right[...], (((0,), (0,)), ((), ())), preferred_element_type=jnp.float32
-    )
-
-
-def weight_grad_of(normed, grads):
-    rows, features = normed.shape
+    out[0] = jnp.dot(left[...], right[...], preferred_element_type=jnp.float32)
+
+
+def weight_grad_of(normed_t, grads):
+    features, rows = normed_t.shape
     tile = grads.shape[1] // 3
     width = 256 if features % 256 == 0 else features
     return pl.pallas_call(
@@ -416,11 +418,11 @@
         grid=(3, features // width),
         out_shape=jax.ShapeDtypeStruct((3, features, tile), jnp.float32),
         in_specs=[
-            pl.BlockSpec((rows, width), lambda s, f: (0, f)),
+            pl.BlockSpec((width, rows), lambda s, f: (f, 0)),
             pl.BlockSpec((rows, tile), lambda s, f: (0, s)),
         ],
         out_specs=pl.BlockSpec((1, width, tile), lambda s, f: (s, f, 0)),
-    )(normed, grads)
+    )(normed_t, grads)
 
 
 def layer_norm(values):
@@ -485,7 +487,7 @@
 def local(n, n_mp, patches, embed_weight, project_weight, patch_counts, segment_ids, targets):
     counts = jnp.broadcast_to(jnp.sum(patch_counts).astype(jnp.float32), (8, 128))
     row_total = patches.shape[0]
-    normed, projected, total = project(
+    normed_t, projected, total = project(
         patches, embed_weight, jnp.transpose(project_weight, (1, 0, 2)), counts, n, n_mp
     )
     patch_total = total[0, 0]
@@ -504,9 +506,7 @@
         grad_rows.reshape(row_total, -1), jnp.broadcast_to(squared_sum, (8, 128)), n, n_mp
     )
     loss_value = squares[0, 0] / (2.0 * patch_total)
-    weight_grad = weight_grad_of(
-        normed.reshape(-1, normed.shape[2]), gathered.reshape(-1, gathered.shape[2])
-    )
+    weight_grad = weight_grad_of(normed_t, gathered.reshape(-1, gathered.shape[2]))
     return (jnp.transpose(weight_grad, (1, 0, 2)), loss_value)
 
 

time: 147 us -> 147 us (level)
  no operation moved by 1% of the time
where the time goes in v3:
time: 147 us; the launch traced here: 146 us
  Pallas kernels  126 us (86%)
  local copies, waits for them, and re-layouts  9.69 us (7%)
  other arithmetic  4.75 us (3%)
  between operations  3.89 us (3%)
  matrix products  1.63 us (1%)
    pallas_call x1, Pallas kernels, project(): pl.pallas_call(functools.partial(project_kernel, n, n_mp), out_shape=(jax...  80.7 us
    pallas_call x1, Pallas kernels, spread(): pl.pallas_call(functools.partial(spread_kernel, n, n_mp, chunks), out_sha...  33.9 us
    pallas_call x1, Pallas kernels, weight_grad_of(): pl.pallas_call(weight_grad_kernel, grid=(3, features // width), out_shape...  11.4 us

profile of v3, /device:TPU:0, one launch (start us, length us, event | category | flops | bytes accessed | tf_op | source)
XLA Modules:
  0.0 145.9 jit_solution(1898591806127752929)
XLA Ops:
  0.6 1.3 reduce_sum.105
  2.6 0.7 broadcast_compare_fusion
  3.2 0.6 broadcast_in_dim.70.counts
  3.8 0.8 compare_and_fusion
  4.6 1.7 %copy.23.patches = bf16[128,588]{1,0:T(8,128)(2,1)} copy(bf16[128,588]{0,1:T(8,128)(2,1)} %param.6) | data formatting | bytes 301056 | tf_op args[0]
  6.4 1.1 copy.28
  7.5 80.7 %shard_map.77 = (bf16[768,1024]{1,0:T(8,128)(2,1)}, f32[128,2304]{1,0:T(8,128)}, f32[8,128]{1,0:T(8,128)}) custom-call(bf16[128,588]{1,0:T(8,128)(2,1)} %copy.23.patches, bf16[192,588]{1,0:T(8,128)(2,1)} %embed.1, bf16[3,768,768]{2,1,0:T(8,128)(2,1)} %bitcast.89, f32[8,128]{1,0:T(8,128)} %broadcast_in_dim.70.counts), custom_call_target="tpu_custom_call" | custom-call | tf_op jit(solution)/shard_map/pallas_call | solution.py:250
  88.2 1.2 slice.19
  90.0 1.6 %copy.24 = f32[128,2304]{0,1:T(8,128)S(1)} copy(f32[128,2304]{1,0:T(8,128)} %get-tuple-element.8) | data formatting | bytes 2359296 | tf_op jit(solution)/shard_map/pallas_call | solution.py:250
  91.7 0.1 multiply_reduce_fusion.4
  91.8 0.3 fusion.34
  92.2 0.2 fusion.24
  92.4 1.4 multiply_reduce_fusion.1
  93.8 1.2 broadcast_in_dim.81.squares
  95.0 0.3 fusion.7
  95.3 0.3 fusion.22
  95.5 0.3 multiply_reduce_fusion.3
  95.8 0.3 fusion.26
  96.2 0.2 fusion.17
  96.4 0.1 fusion.18
  96.6 1.1 copy.34.grads
  97.7 33.9 %shard_map.78 = (bf16[8,128,2304]{2,1,0:T(8,128)(2,1)}, f32[8,128]{1,0:T(8,128)}) custom-call(bf16[128,2304]{1,0:T(8,128)(2,1)} %copy.34.grads, f32[8,128]{1,0:T(8,128)} %broadcast_in_dim.81.squares), custom_call_target="tpu_custom_call" | custom-call | tf_op jit(solution)/shard_map/pallas_call | solution.py:384
  131.5 1.2 slice.20
  133.4 11.4 %shard_map.79 = f32[3,768,768]{2,1,0:T(8,128)} custom-call(bf16[768,1024]{1,0:T(8,128)(2,1)} %get-tuple-element.7.left, bf16[1024,2304]{1,0:T(8,128)(2,1)} %bitcast.88), custom_call_target="tpu_custom_call" | custom-call | tf_op jit(solution)/shard_map/pallas_call | solution.py:416
  (11 shorter events, 0.2 us)

commit v4 on v3

--- a/solution.py
+++ b/solution.py
@@ -412,16 +412,16 @@
 def weight_grad_of(normed_t, grads):
     features, rows = normed_t.shape
     tile = grads.shape[1] // 3
-    width = 256 if features % 256 == 0 else features
+    half = tile // 2 if tile % 256 == 0 else tile
     return pl.pallas_call(
         weight_grad_kernel,
-        grid=(3, features // width),
+        grid=(3, tile // half),
         out_shape=jax.ShapeDtypeStruct((3, features, tile), jnp.float32),
         in_specs=[
-            pl.BlockSpec((width, rows), lambda s, f: (f, 0)),
-            pl.BlockSpec((rows, tile), lambda s, f: (0, s)),
+            pl.BlockSpec((features, rows), lambda s, f: (0, 0)),
+            pl.BlockSpec((rows, half), lambda s, f: (0, s * (tile // half) + f)),
         ],
-        out_specs=pl.BlockSpec((1, width, tile), lambda s, f: (s, f, 0)),
+        out_specs=pl.BlockSpec((1, features, half), lambda s, f: (s, 0, f)),
     )(normed_t, grads)
 
 

time: 147 us -> 145 us (0.986)
  Pallas kernels: 126 us -> 124 us
    pallas_call x1, Pallas kernels: 11.4 us -> 9.9 us  [weight_grad_of(): pl.pallas_call(weight_grad_kernel, grid=(3, tile // half), out_shape=jax....]
where the time goes in v4:
time: 145 us; the launch traced here: 144 us
  Pallas kernels  124 us (86%)
  local copies, waits for them, and re-layouts  9.69 us (7%)
  other arithmetic  4.75 us (3%)
  between operations  3.89 us (3%)
  matrix products  1.63 us (1%)
    pallas_call x1, Pallas kernels, project(): pl.pallas_call(functools.partial(project_kernel, n, n_mp), out_shape=(jax...  80.7 us
    pallas_call x1, Pallas kernels, spread(): pl.pallas_call(functools.partial(spread_kernel, n, n_mp, chunks), out_sha...  33.9 us
    pallas_call x1, Pallas kernels, weight_grad_of(): pl.pallas_call(weight_grad_kernel, grid=(3, tile // half), out_shape=jax....  9.9 us

profile of v4, /device:TPU:0, one launch (start us, length us, event | category | flops | bytes accessed | tf_op | source)
XLA Modules:
  0.0 144.4 jit_solution(15875614958442216185)
XLA Ops:
  0.6 1.3 reduce_sum.105
  2.6 0.7 broadcast_compare_fusion
  3.2 0.6 broadcast_in_dim.70.counts
  3.8 0.8 compare_and_fusion
  4.6 1.7 %copy.23.patches = bf16[128,588]{1,0:T(8,128)(2,1)} copy(bf16[128,588]{0,1:T(8,128)(2,1)} %param.6) | data formatting | bytes 301056 | tf_op args[0]
  6.4 1.1 copy.28
  7.5 80.7 %shard_map.77 = (bf16[768,1024]{1,0:T(8,128)(2,1)}, f32[128,2304]{1,0:T(8,128)}, f32[8,128]{1,0:T(8,128)}) custom-call(bf16[128,588]{1,0:T(8,128)(2,1)} %copy.23.patches, bf16[192,588]{1,0:T(8,128)(2,1)} %embed.1, bf16[3,768,768]{2,1,0:T(8,128)(2,1)} %bitcast.89, f32[8,128]{1,0:T(8,128)} %broadcast_in_dim.70.counts), custom_call_target="tpu_custom_call" | custom-call | tf_op jit(solution)/shard_map/pallas_call | solution.py:250
  88.2 1.2 slice.19
  90.0 1.6 %copy.24 = f32[128,2304]{0,1:T(8,128)S(1)} copy(f32[128,2304]{1,0:T(8,128)} %get-tuple-element.8) | data formatting | bytes 2359296 | tf_op jit(solution)/shard_map/pallas_call | solution.py:250
  91.7 0.1 multiply_reduce_fusion.4
  91.8 0.3 fusion.34
  92.2 0.2 fusion.24
  92.4 1.4 multiply_reduce_fusion.1
  93.8 1.2 broadcast_in_dim.81.squares
  95.0 0.3 fusion.7
  95.3 0.3 fusion.22
  95.5 0.3 multiply_reduce_fusion.3
  95.8 0.3 fusion.26
  96.2 0.2 fusion.17
  96.4 0.1 fusion.18
  96.6 1.1 copy.34.grads
  97.7 33.9 %shard_map.78 = (bf16[8,128,2304]{2,1,0:T(8,128)(2,1)}, f32[8,128]{1,0:T(8,128)}) custom-call(bf16[128,2304]{1,0:T(8,128)(2,1)} %copy.34.grads, f32[8,128]{1,0:T(8,128)} %broadcast_in_dim.81.squares), custom_call_target="tpu_custom_call" | custom-call | tf_op jit(solution)/shard_map/pallas_call | solution.py:384
  131.5 1.2 slice.20
  133.4 9.9 %shard_map.79 = f32[3,768,768]{2,1,0:T(8,128)} custom-call(bf16[768,1024]{1,0:T(8,128)(2,1)} %get-tuple-element.7.left, bf16[1024,2304]{1,0:T(8,128)(2,1)} %bitcast.88), custom_call_target="tpu_custom_call" | custom-call | tf_op jit(solution)/shard_map/pallas_call | solution.py:416
  (11 shorter events, 0.2 us)
